TPU v7x, 32 devices: a whole 2x2x4 slice. The times are simulated.
32 devices in a mesh: group: 4 (over y, core), blk: 8 (over z, x).
Axes of the slice: x: 2, y: 2, z: 4, core: 2. Of those that a mesh axis runs over, the one named last changes fastest.
Arguments:
- features: bfloat16 [1024, 2048], P('blk', 'group'), may hold values from -6 to 6
- weight: bfloat16 [2048, 256], P('group'), may hold values from -0.125 to 0.125
- queue: bfloat16 [16384, 256], P(('group', 'blk')), may hold values from -0.5 to 0.5, as said below
- fresh_keys: bfloat16 [1024, 256], P('blk'), may hold values from -0.3984375 to 0.3984375
- positives: int32 [1024], P('blk'), may hold values from 0 to 1023, each once
- write_slot: int32 [1], replicated, may hold values from 0 to 15360
Outputs:
- query_loss: float32 [1024], P('blk')
- weight_grad: float32 [2048, 256], P(('group', 'blk'))
- new_queue: bfloat16 [16384, 256], P(('group', 'blk'))
Inputs may be any that keep to these rules, and one draw needn't show every extreme that they name: `queue`: scaled item keys.
All inputs are finite; a program needn't handle non-finite values.
Results may differ from a plain program's by a relative error of at most 0.003.
The roundings to bfloat16 on the way count: a program that leaves them out, or rounds other values in their place, can miss the bound.
Values may be sent and summed in bfloat16 or wider, within the bound.
No kernel may reach another device: no remote copies, remote signals or barrier semaphores. Data moves between devices by JAX's collectives and lax.ppermute only.
A program may use at most 64 MiB of HBM per device.

v0:
```python
import jax
import jax.numpy as jnp
from jax import lax
from jax.sharding import PartitionSpec as P

epsilon = 1e-06
inverse_sharpness_factor = 8.0


def local(features, weight, queue, fresh_keys, positives, write_slot):
    partial_proj = jnp.dot(features, weight, preferred_element_type=jnp.float32)
    projected = lax.psum(partial_proj, "group")
    length = jnp.sqrt(jnp.sum(projected * projected, axis=1, keepdims=True) + epsilon)
    unit_rows = projected / length
    query_rows = unit_rows.astype(jnp.bfloat16)
    all_fresh = lax.all_gather(fresh_keys, "blk", axis=0, tiled=True)
    all_queries = lax.all_gather(query_rows, "blk", axis=0, tiled=True)
    query_total = all_queries.shape[0]
    key_width = all_queries.shape[1]
    blk_count = lax.axis_size("blk")
    block_rows = 512
    query_blocks = all_queries.reshape(query_total // block_rows, block_rows, key_width)

    def score_block(carry, rows_now):
        similarity_matrix = jnp.einsum(
            "qc,sc->qs", rows_now, queue, preferred_element_type=jnp.float32
        )
        exponentials = jnp.exp(inverse_sharpness_factor * similarity_matrix)
        denominator = jnp.sum(exponentials, axis=1)
        numerator = jnp.dot(
            exponentials.astype(jnp.bfloat16), queue, preferred_element_type=jnp.float32
        )
        return (carry, (numerator, denominator))

    _, (numer_blocks, denom_blocks) = lax.scan(score_block, jnp.float32(0.0), query_blocks)
    numer_all = numer_blocks.reshape(query_total, key_width)
    denom_all = denom_blocks.reshape(query_total)
    numer_part, denom_part = (
        lax.psum_scatter(numer_all, "blk", scatter_dimension=0, tiled=True),
        lax.psum_scatter(denom_all, "blk", scatter_dimension=0, tiled=True),
    )
    numerator, denominator = lax.psum((numer_part, denom_part), "group")
    paired_encodings = jnp.take(all_fresh, positives, axis=0).astype(jnp.float32)
    pair_score = inverse_sharpness_factor * jnp.sum(
        query_rows.astype(jnp.float32) * paired_encodings, axis=1
    )
    pair_weight = jnp.exp(pair_score)
    probability_mass = pair_weight + denominator
    query_loss = jnp.log(probability_mass) - pair_score
    query_derivative = inverse_sharpness_factor * (
        (pair_weight[:, None] * paired_encodings + numerator) / probability_mass[:, None]
        - paired_encodings
    )
    along = jnp.sum(query_derivative * unit_rows, axis=1, keepdims=True)
    grad_projected = ((query_derivative - along * unit_rows) / length).astype(jnp.bfloat16)
    weight_grad = lax.psum_scatter(
        lax.dot_general(
            features, grad_projected, (((0,), (0,)), ((), ())), preferred_element_type=jnp.float32
        ),
        "blk",
        scatter_dimension=0,
        tiled=True,
    )
    slot_count = queue.shape[0]
    device_index = lax.axis_index("group") * blk_count + lax.axis_index("blk")
    window_start = write_slot[0]
    slot_index = device_index * slot_count + jnp.arange(slot_count, dtype=jnp.int32)
    offset = slot_index - window_start
    in_window = (offset >= 0) & (offset < query_total)
    picked = jnp.take(all_fresh, jnp.clip(offset, 0, query_total - 1), axis=0)
    new_queue = jnp.where(in_window[:, None], picked, queue)
    return (query_loss, weight_grad, new_queue)


def solution(mesh):
    in_specs = (
        P("blk", "group"),
        P("group", None),
        P(("group", "blk"), None),
        P("blk", None),
        P("blk"),
        P(),
    )
    out_specs = (P("blk"), P(("group", "blk"), None), P(("group", "blk"), None))
    return jax.shard_map(local, mesh=mesh, in_specs=in_specs, out_specs=out_specs, check_vma=False)
```

profile of v0, /device:TPU:0, one launch (start us, length us, event | category | flops | bytes accessed | tf_op | source)
XLA Modules:
  0.0 252.1 jit_solution(920039892036683181)
XLA Ops:
  7.2 0.0 copy-start
  7.2 0.0 all-reduce.4.cloned.1.call-start
  7.2 0.9 copy-done
  8.1 1.7 fusion.20
  9.9 0.0 copy-start.7
  9.9 0.0 copy-start.6
  9.9 0.0 all-reduce.4.cloned.1.call-update
  9.9 0.0 reduce-scatter.5.cloned.1.call-start
  9.9 0.6 copy-done.7
  10.6 0.2 copy-done.6
  10.7 33.0 %all_gather.6 = bf16[1024,256]{1,0:T(8,128)(2,1)S(1)} all-gather(bf16[128,256]{1,0:T(8,128)(2,1)S(1)} %copy-done.6), channel_id=1, replica_groups=mesh['group'=4,'blk'=8] {'blk'}, dimensions={0}, use_global_device_ids=true | all-gather | bytes 589824 | tf_op jit(solution)/shard_map/all_gather | solution.py:16
  43.8 0.8 gather_fusion
  44.6 0.8 all-reduce.4.cloned.1.call-done
  45.4 0.0 copy-start.2
  45.4 1.1 multiply_reduce_fusion.1
  46.5 0.0 copy-done.2
  46.5 0.2 fusion.6
  46.7 0.0 copy-start.1
  46.7 31.5 %all_gather.7 = bf16[1024,256]{1,0:T(8,128)(2,1)S(1)} all-gather(bf16[128,256]{1,0:T(8,128)(2,1)S(1)} %get-tuple-element.53), channel_id=1, replica_groups=mesh['group'=4,'blk'=8] {'blk'}, dimensions={0}, use_global_device_ids=true | all-gather | bytes 589824 | tf_op jit(solution)/shard_map/all_gather | solution.py:17
  78.2 0.0 copy-done.1
  78.2 1.6 while.12
  78.3 0.4 fusion.35
  78.7 0.3 fusion.36
  79.0 0.4 fusion.35
  79.5 0.3 fusion.36
  79.8 0.0 copy-start.3
  79.8 1.0 copy-done.3
  80.8 0.0 reduce-scatter.5.cloned.1.call-update
  80.8 0.0 all-reduce.6.cloned.1.call-start
  80.9 0.0 copy-start.8
  80.9 0.6 copy-done.8
  81.6 0.6 dynamic-slice
  82.8 21.5 %all-reduce = f32[1024]{0:T(1024)S(1)} all-reduce(f32[1024]{0:T(1024)S(1)} %bitcast.43), channel_id=2, replica_groups=mesh['group'=4,'blk'=8] {'blk'}, use_global_device_ids=true, to_apply=%region_6.7.clone | all-reduce | flops 1024 | bytes 8192
  104.3 0.1 dynamic-slice.1
  104.4 6.0 %psum.22 = f32[128]{0:T(128)S(1)} all-reduce(f32[128]{0:T(128)S(1)} %dynamic-slice.1), channel_id=1, replica_groups=mesh['group'=4,'blk'=8] {'group'}, use_global_device_ids=true, to_apply=%region_7.8 | all-reduce | flops 128 | bytes 1024 | tf_op jit(solution)/shard_map/psum | solution.py:42
  110.4 35.3 %reduce-scatter.5.cloned.1.call-done = f32[128,256]{1,0:T(8,128)} async-done(((f32[1024,256]{1,0:T(8,128)}), f32[128,256]{1,0:T(8,128)}) %reduce-scatter.5.cloned.1.call-update) | async-done | bytes 131088 | tf_op jit(solution)/shard_map/reduce_scatter | solution.py:39
  145.7 0.0 all-reduce.6.cloned.1.call-update
  145.7 0.0 reduce-scatter.7.cloned.1.call-start
  145.7 0.5 fusion.15
  146.3 32.4 %all-reduce.6.cloned.1.call-done = f32[128,256]{1,0:T(8,128)} async-done(((f32[128,256]{1,0:T(8,128)}), f32[128,256]{1,0:T(8,128)}) %all-reduce.6.cloned.1.call-update) | async-done | bytes 131088 | tf_op jit(solution)/shard_map/psum | solution.py:42
  178.7 0.0 copy-start.4
  178.7 0.0 copy-start.5
  178.7 1.2 multiply_reduce_fusion
  179.9 0.0 copy-done.4
  179.9 0.0 copy-done.5
  179.9 0.4 convolution_bitcast_fusion.1
  180.3 1.0 copy.12
  181.3 0.0 reduce-scatter.7.cloned.1.call-update
  182.0 2.0 gather_fusion.1
  184.0 0.9 select_select_fusion
  184.9 60.7 %reduce-scatter.7.cloned.1.call-done = f32[64,256]{1,0:T(8,128)} async-done(((f32[512,256]{1,0:T(8,128)}), f32[64,256]{1,0:T(8,128)}) %reduce-scatter.7.cloned.1.call-update) | async-done | bytes 65552
  (12 shorter events, 0.1 us)
Async XLA Ops:
  7.2 1.0 copy-start
  7.2 38.2 %all-reduce.4.cloned.1.call-start = ((), (), s32[]{:S(2)}) async-start(), calls=%async_computation.2 | async-start | bytes 262144 | tf_op jit(solution)/shard_map/psum | solution.py:12
  9.9 0.7 copy-start.7
  9.9 0.9 copy-start.6
  9.9 135.8 %reduce-scatter.5.cloned.1.call-start = ((), (), s32[]{:S(2)}) async-start(), calls=%async_computation.3 | async-start | bytes 1179648 | tf_op jit(solution)/shard_map/reduce_scatter | solution.py:39
  45.4 1.1 copy-start.2
  46.7 31.5 %copy-start.1 = (bf16[512,256]{1,0:T(8,128)(2,1)S(1)}, bf16[512,256]{1,0:T(8,128)(2,1)}, u32[]{:S(2)}) copy-start(bf16[512,256]{1,0:T(8,128)(2,1)} %param.10) | copy-start | bytes 786436
  79.8 1.0 copy-start.3
  80.8 97.9 %all-reduce.6.cloned.1.call-start = ((), (), s32[]{:S(2)}) async-start(), calls=%async_computation.4 | async-start | bytes 262144 | tf_op jit(solution)/shard_map/psum | solution.py:42
  80.9 0.7 copy-start.8
  145.7 99.9 %reduce-scatter.7.cloned.1.call-start = ((), (), s32[]{:S(2)}) async-start(), calls=%async_computation.5 | async-start | bytes 589824
  178.7 1.2 copy-start.4
  178.7 1.2 copy-start.5
Sparse Core Ops, SparseCore 0:
  10.9 34.4 all-reduce.3
  81.0 64.6 reduce-scatter.4
  148.0 30.6 all-reduce.5
  182.5 63.0 reduce-scatter.6
where the time goes:
time: 252 us
  waiting for transfers between devices  129 us (51%)
  blocking collectives  92.1 us (37%)
  between operations  15.2 us (6%)
  local copies, waits for them, and re-layouts  7.85 us (3%)
  other arithmetic  3.94 us (2%)
  matrix products  3.58 us (1%)
    unnamed x5, waiting for transfers between devices  60.7 us
    reduce_scatter x1, waiting for transfers between devices, local(): lax.psum_scatter(numer_all, 'blk', scatter_dimension=0, tiled=True)  35.3 us
    all_gather x1, blocking collectives, local(): all_fresh = lax.all_gather(fresh_keys, 'blk', axis=0, tiled=True)  33 us
    psum x1, waiting for transfers between devices, local(): numerator, denominator = lax.psum((numer_part, denom_part), 'group')  32.4 us
    all_gather x1, blocking collectives, local(): all_queries = lax.all_gather(query_rows, 'blk', axis=0, tiled=True)  31.5 us
    unnamed x1, blocking collectives  21.5 us
    psum x1, blocking collectives, local(): numerator, denominator = lax.psum((numer_part, denom_part), 'group')  6.03 us
  transfers between devices with their start and end apart: 4, of which 4 were waited for; matrix products, arithmetic and copies ran while one was open for 2% of the time, Pallas kernels for 0%

commit v1 on v0

--- a/solution.py
+++ b/solution.py
@@ -13,8 +13,13 @@
     length = jnp.sqrt(jnp.sum(projected * projected, axis=1, keepdims=True) + epsilon)
     unit_rows = projected / length
     query_rows = unit_rows.astype(jnp.bfloat16)
-    all_fresh = lax.all_gather(fresh_keys, "blk", axis=0, tiled=True)
-    all_queries = lax.all_gather(query_rows, "blk", axis=0, tiled=True)
+    all_fresh, all_queries = jnp.split(
+        lax.all_gather(
+            jnp.concatenate([fresh_keys, query_rows], axis=1), "blk", axis=0, tiled=True
+        ),
+        [fresh_keys.shape[1]],
+        axis=1,
+    )
     query_total = all_queries.shape[0]
     key_width = all_queries.shape[1]
     blk_count = lax.axis_size("blk")

time: 252 us -> 262 us (1.040)
  waiting for transfers between devices: 129 us -> 204 us
  blocking collectives: 92.1 us -> 25.4 us
    all_gather x2 -> x0, blocking collectives: 64.6 us -> none  [the longest x1 33 us: local(): all_fresh = lax.all_gather(fresh_keys, 'blk', axis=0, tiled=True)]
    all_gather x0 -> x1, waiting for transfers between devices: none -> 40.4 us  [local(): lax.all_gather(jnp.concatenate([fresh_keys, query_rows], axis=1), 'blk',...]
    psum x1, waiting for transfers between devices: 0.8 us -> 35.5 us  [local(): projected = lax.psum(partial_proj, 'group')]
    unnamed x5 -> x6, waiting for transfers between devices: 60.7 us -> 60.7 us
  transfers between devices with their start and end apart: 4 -> 5, of which waited for: 4 -> 5; matrix products, arithmetic and copies ran while one was open for 2% -> 2% of each run, Pallas kernels for 0% -> 0%
where the time goes in v1:
time: 262 us
  waiting for transfers between devices  204 us (78%)
  blocking collectives  25.4 us (10%)
  between operations  15.3 us (6%)
  local copies, waits for them, and re-layouts  9.11 us (3%)
  other arithmetic  4.7 us (2%)
  matrix products  3.57 us (1%)
    unnamed x6, waiting for transfers between devices  60.7 us
    all_gather x1, waiting for transfers between devices, local(): lax.all_gather(jnp.concatenate([fresh_keys, query_rows], axis=1), 'blk',...  40.4 us
    psum x1, waiting for transfers between devices, local(): projected = lax.psum(partial_proj, 'group')  35.5 us
    reduce_scatter x1, waiting for transfers between devices, local(): lax.psum_scatter(numer_all, 'blk', scatter_dimension=0, tiled=True)  35 us
    psum x1, waiting for transfers between devices, local(): numerator, denominator = lax.psum((numer_part, denom_part), 'group')  32.3 us
    unnamed x1, blocking collectives  19.3 us
    psum x1, blocking collectives, local(): numerator, denominator = lax.psum((numer_part, denom_part), 'group')  6.03 us
  transfers between devices with their start and end apart: 5, of which 5 were waited for; matrix products, arithmetic and copies ran while one was open for 2% of the time, Pallas kernels for 0%

profile of v1, /device:TPU:0, one launch (start us, length us, event | category | flops | bytes accessed | tf_op | source)
XLA Modules:
  0.0 262.2 jit_solution(3720959258961611828)
XLA Ops:
  7.2 0.0 copy-start
  7.2 0.0 all-reduce.4.cloned.1.call-start
  7.2 0.9 copy-done
  8.1 1.7 fusion.20
  9.9 0.0 all-reduce.4.cloned.1.call-update
  9.9 0.0 all-gather.2.cloned.1.call-start
  9.9 35.5 %all-reduce.4.cloned.1.call-done = f32[128,256]{1,0:T(8,128)} async-done(((f32[128,256]{1,0:T(8,128)}), f32[128,256]{1,0:T(8,128)}) %all-reduce.4.cloned.1.call-update) | async-done | bytes 131088 | tf_op jit(solution)/shard_map/psum | solution.py:12
  45.4 0.0 copy-start.2
  45.4 1.1 multiply_reduce_fusion.1
  46.5 0.0 copy-done.2
  46.5 0.0 copy-start.6
  46.5 0.1 fusion.16
  46.6 0.7 copy-done.6
  47.4 0.7 pad_maximum_fusion
  48.0 0.0 all-gather.2.cloned.1.call-update
  48.1 0.0 reduce-scatter.5.cloned.1.call-start
  48.1 0.0 copy-start.1
  48.1 40.4 %all-gather.2.cloned.1.call-done = bf16[1024,512]{1,0:T(8,128)(2,1)} async-done(((bf16[128,512]{1,0:T(8,128)(2,1)}), bf16[1024,512]{1,0:T(8,128)(2,1)}) %all-gather.2.cloned.1.call-update) | async-done | bytes 1048592 | tf_op jit(solution)/shard_map/all_gather | solution.py:17
  88.5 1.3 fusion.19
  89.8 0.0 copy-done.1
  89.8 1.6 while.12
  89.8 0.4 fusion.35
  90.2 0.3 fusion.36
  90.6 0.4 fusion.35
  91.0 0.3 fusion.36
  91.4 0.0 copy-start.3
  91.4 1.0 copy-done.3
  92.3 0.0 reduce-scatter.5.cloned.1.call-update
  92.4 0.0 all-reduce.6.cloned.1.call-start
  92.4 0.0 copy-start.8
  92.4 0.6 copy-done.8
  93.1 0.6 dynamic-slice
  93.7 0.0 copy-start.7
  94.3 0.0 copy-done.7
  94.4 0.8 gather_fusion
  95.2 19.3 %all-reduce = f32[1024]{0:T(1024)S(1)} all-reduce(f32[1024]{0:T(1024)S(1)} %bitcast.43), channel_id=2, replica_groups=mesh['group'=4,'blk'=8] {'blk'}, use_global_device_ids=true, to_apply=%region_6.7.clone | all-reduce | flops 1024 | bytes 8192
  114.6 0.1 dynamic-slice.1
  114.7 6.0 %psum.22 = f32[128]{0:T(128)S(1)} all-reduce(f32[128]{0:T(128)S(1)} %dynamic-slice.1), channel_id=1, replica_groups=mesh['group'=4,'blk'=8] {'group'}, use_global_device_ids=true, to_apply=%region_7.8 | all-reduce | flops 128 | bytes 1024 | tf_op jit(solution)/shard_map/psum | solution.py:47
  120.7 0.2 fusion.6
  120.9 35.0 %reduce-scatter.5.cloned.1.call-done = f32[128,256]{1,0:T(8,128)} async-done(((f32[1024,256]{1,0:T(8,128)}), f32[128,256]{1,0:T(8,128)}) %reduce-scatter.5.cloned.1.call-update) | async-done | bytes 131088 | tf_op jit(solution)/shard_map/reduce_scatter | solution.py:44
  155.8 0.0 all-reduce.6.cloned.1.call-update
  155.9 0.0 reduce-scatter.7.cloned.1.call-start
  155.9 0.5 fusion.15
  156.4 32.3 %all-reduce.6.cloned.1.call-done = f32[128,256]{1,0:T(8,128)} async-done(((f32[128,256]{1,0:T(8,128)}), f32[128,256]{1,0:T(8,128)}) %all-reduce.6.cloned.1.call-update) | async-done | bytes 131088 | tf_op jit(solution)/shard_map/psum | solution.py:47
  188.8 0.0 copy-start.4
  188.8 0.0 copy-start.5
  188.8 1.2 multiply_reduce_fusion
  190.0 0.0 copy-done.4
  190.0 0.0 copy-done.5
  190.0 0.4 convolution_bitcast_fusion.1
  190.4 1.0 copy.12
  191.4 0.0 reduce-scatter.7.cloned.1.call-update
  192.1 2.0 gather_fusion.1
  194.0 0.9 select_select_fusion
  195.0 60.7 %reduce-scatter.7.cloned.1.call-done = f32[64,256]{1,0:T(8,128)} async-done(((f32[512,256]{1,0:T(8,128)}), f32[64,256]{1,0:T(8,128)}) %reduce-scatter.7.cloned.1.call-update) | async-done | bytes 65552
  (12 shorter events, 0.1 us)
Async XLA Ops:
  7.2 1.0 copy-start
  7.2 38.2 %all-reduce.4.cloned.1.call-start = ((), (), s32[]{:S(2)}) async-start(), calls=%async_computation.2 | async-start | bytes 262144 | tf_op jit(solution)/shard_map/psum | solution.py:12
  9.9 78.6 %all-gather.2.cloned.1.call-start = ((), (), s32[]{:S(2)}) async-start(), calls=%async_computation.3 | async-start | bytes 1179648 | tf_op jit(solution)/shard_map/all_gather | solution.py:17
  45.4 1.1 copy-start.2
  46.5 0.8 copy-start.6
  48.1 107.8 %reduce-scatter.5.cloned.1.call-start = ((), (), s32[]{:S(2)}) async-start(), calls=%async_computation.4 | async-start | bytes 1179648 | tf_op jit(solution)/shard_map/reduce_scatter | solution.py:44
  48.1 41.6 %copy-start.1 = (bf16[512,256]{1,0:T(8,128)(2,1)S(1)}, bf16[512,256]{1,0:T(8,128)(2,1)}, u32[]{:S(2)}) copy-start(bf16[512,256]{1,0:T(8,128)(2,1)} %param.10) | copy-start | bytes 786436
  91.4 1.0 copy-start.3
  92.4 96.4 %all-reduce.6.cloned.1.call-start = ((), (), s32[]{:S(2)}) async-start(), calls=%async_computation.5 | async-start | bytes 262144 | tf_op jit(solution)/shard_map/psum | solution.py:47
  92.4 0.7 copy-start.8
  93.7 0.7 copy-start.7
  155.9 99.8 %reduce-scatter.7.cloned.1.call-start = ((), (), s32[]{:S(2)}) async-start(), calls=%async_computation.6 | async-start | bytes 589824
  188.8 1.2 copy-start.4
  188.8 1.2 copy-start.5
Sparse Core Ops, SparseCore 0:
  10.9 34.4 all-reduce.3
  48.2 40.2 all-gather.1
  92.5 63.2 reduce-scatter.4
  158.0 30.7 all-reduce.5
  192.5 63.0 reduce-scatter.6
